TPU v7x, 512 devices: a whole 4x8x8 slice. The times are simulated.
512 devices in a mesh: gx: 32 (over y_lo, z), gy: 16 (over y_hi, x, core).
Axes of the slice: x: 4, y: 8 (y_hi: 2, y_lo: 4; y = y_hi * 4 + y_lo), z: 8, core: 2. Of those that a mesh axis runs over, the one named last changes fastest.
Arguments:
- duals: float32 [16, 64, 64, 128], P(None, 'gx', 'gy'), may hold values from -6 to 6
- residual: float32 [16, 64, 64, 128], P(None, 'gx', 'gy')
- direction: float32 [16, 64, 64, 128], P(None, 'gx', 'gy'), may hold values from -6 to 6
- prev_rho: float32 [16], replicated, may hold values from 262144 to 1048576
- dual_schur: float32 [64, 64, 256, 256], P('gx', 'gy'), as said below
- coupling: float32 [64, 64, 8, 256], P('gx', 'gy'), may hold values from -0.75 to 0.75
- coarse_inverse: float32 [32, 384, 384], P('gx'), as said below
- edge_map: int32 [64, 64, 256], P('gx', 'gy'), may hold values from 0 to 255, each once within a row
- corner_slot: int32 [64, 64, 8], P('gx', 'gy'), may hold values from 0 to 384, as said below
- active: int32 [64, 64, 128], P('gx', 'gy'), may hold values 0 or 1
- scaling: float32 [64, 64, 128], P('gx', 'gy'), may hold values from 0.25 to 1
Outputs:
- new_duals: float32 [16, 64, 64, 128], P(None, 'gx', 'gy')
- new_residual: float32 [16, 64, 64, 128], P(None, 'gx', 'gy')
- new_direction: float32 [16, 64, 64, 128], P(None, 'gx', 'gy')
Inputs may be any that keep to these rules, and one draw needn't show every extreme that they name: Each subdomain's block of dual_schur and each region's block of coarse_inverse is symmetric positive definite. `coarse_inverse`: each region's block is symmetric positive definite. `corner_slot`: slots number the corner dofs of a region; a corner shared by subdomains of one region has one slot; 384 marks corners on the clamped bottom edge, which have no dof.
All inputs are finite; a program needn't handle non-finite values. No bound on the sum of `active` on one device may be relied on, other than what follows from the above.
Results may differ from a plain program's by a relative error of at most 0.00014.
Values sent between devices are 32-bit elements; how exact they have to be, the bound alone decides.
A program may use at most 64 MiB of HBM per device.

v0:
```python
import jax
import jax.numpy as jnp
from jax import lax
from jax.sharding import PartitionSpec as P

ITERS = 6


def passed_along(value, axis, by):
    peers = lax.axis_size(axis)
    pairs = [(i, i + by) for i in range(peers) if 0 <= i + by < peers]
    return lax.ppermute(value, axis, pairs)


def across_x(slab, offset):
    return passed_along(slab, "gx", offset)


def across_y(slab, offset):
    return passed_along(slab, "gy", offset)


def case_sum(values):
    return lax.psum(values, ("gx", "gy"))


def shards(
    duals,
    residual,
    direction,
    prev_rho,
    dual_schur,
    coupling,
    coarse_inverse,
    edge_map,
    corner_slot,
    active,
    scaling,
):
    high = lax.Precision.HIGHEST
    cases, span_x, span_y, owned = duals.shape
    half = owned // 2
    width_c = coarse_inverse.shape[-1]
    columns = lax.axis_index("gx") * span_x + jnp.arange(span_x)
    rowset = lax.axis_index("gy") * span_y + jnp.arange(span_y)
    east_ok = jnp.broadcast_to(
        (columns < span_x * lax.axis_size("gx") - 1)[:, None, None], (span_x, span_y, half)
    )
    north_ok = jnp.broadcast_to(
        (rowset < span_y * lax.axis_size("gy") - 1)[None, :, None], (span_x, span_y, half)
    )
    keep = active.astype(jnp.float32) * jnp.concatenate([east_ok, north_ok], -1).astype(jnp.float32)
    inverse = jnp.argsort(edge_map, axis=-1)
    onehot = (corner_slot[..., None] == jnp.arange(width_c, dtype=jnp.int32)).astype(jnp.float32)
    region_inv = coarse_inverse[0]
    lam = duals
    res = residual
    pprev = keep * direction
    rho_old = prev_rho
    for step in range(ITERS):
        zvec = keep * scaling * res
        rho = case_sum(jnp.sum(res * zvec, axis=(1, 2, 3)))
        beta = rho / rho_old
        pvec = zvec + beta[:, None, None, None] * pprev
        part_e = pvec[..., :half]
        part_n = pvec[..., half:]
        from_west = across_x(part_e[:, -1].reshape(cases, span_y * half), 1).reshape(
            cases, 1, span_y, half
        )
        west = -jnp.concatenate([from_west, part_e[:, :-1]], 1)
        from_south = across_y(part_n[:, :, -1].reshape(cases, span_x * half), 1).reshape(
            cases, span_x, 1, half
        )
        south = -jnp.concatenate([from_south, part_n[:, :, :-1]], 2)
        edge_vec = jnp.concatenate([west, part_e, south, part_n], -1)
        local = jnp.take_along_axis(edge_vec, edge_map[None], -1)
        work = jnp.einsum("xyij,kxyj->kxyi", dual_schur, local, precision=high)
        corner_val = jnp.einsum("xycj,kxyj->kxyc", coupling, local, precision=high)
        partial_total = jnp.einsum("kxyc,xycn->kn", corner_val, onehot, precision=high)
        total = lax.psum(partial_total, "gy")
        solved = jnp.einsum("nm,km->kn", region_inv, total, precision=high)
        back = jnp.einsum("xycn,kn->kxyc", onehot, solved, precision=high)
        work = work + jnp.einsum("xycj,kxyc->kxyj", coupling, back, precision=high)
        work_edge = jnp.take_along_axis(work, inverse[None], -1)
        west_w = work_edge[..., :half]
        east_w = work_edge[..., half : 2 * half]
        south_w = work_edge[..., 2 * half : 3 * half]
        north_w = work_edge[..., 3 * half :]
        from_east = across_x(west_w[:, 0].reshape(cases, span_y * half), -1).reshape(
            cases, 1, span_y, half
        )
        east_nb = jnp.concatenate([west_w[:, 1:], from_east], 1)
        from_north = across_y(south_w[:, :, 0].reshape(cases, span_x * half), -1).reshape(
            cases, span_x, 1, half
        )
        north_nb = jnp.concatenate([south_w[:, :, 1:], from_north], 2)
        qvec = jnp.concatenate([east_w - east_nb, north_w - north_nb], -1) * keep
        alpha = rho / case_sum(jnp.sum(pvec * qvec, axis=(1, 2, 3)))
        lam = lam + alpha[:, None, None, None] * pvec
        res = res - alpha[:, None, None, None] * qvec
        rho_old = rho
        pprev = pvec
    return (lam, res, pprev)


def solution(mesh):
    placed = (
        P(None, "gx", "gy", None),
        P(None, "gx", "gy", None),
        P(None, "gx", "gy", None),
        P(),
        P("gx", "gy", None, None),
        P("gx", "gy", None, None),
        P("gx", None, None),
        P("gx", "gy", None),
        P("gx", "gy", None),
        P("gx", "gy", None),
        P("gx", "gy", None),
    )
    return jax.shard_map(
        shards,
        mesh=mesh,
        in_specs=placed,
        out_specs=(P(None, "gx", "gy", None), P(None, "gx", "gy", None), P(None, "gx", "gy", None)),
        check_vma=False,
    )
```

profile of v0, /device:TPU:1, one launch (start us, length us, event | category | flops | bytes accessed | tf_op | source)
XLA Modules:
  0.0 2282.1 jit_solution(7444544353813421610)
XLA Ops:
  9.3 106.1 %psum.126 = f32[16]{0:T(128)S(1)} all-reduce(f32[16]{0:T(128)S(1)} %fusion.42), channel_id=1, replica_groups=mesh['gx'=32,'gy'=16] {'gx','gy'}, use_global_device_ids=true, to_apply=%region_1.2 | all-reduce | flops 16 | bytes 128 | tf_op jit(solution)/shard_map/psum | solution.py:24
  117.1 1.8 collective-permute-start
  119.1 3.3 collective-permute-start.1
  124.6 3.3 sort.19.cloned.1.call-done
  131.0 31.7 %gather_fusion = f32[2048,16]{1,0:T(8,128)} fusion(f32[16,2,4,256]{0,3,2,1:T(8,128)} %copy.75, s32[2048]{0:T(1024)S(1)} %bitcast.287), kind=kCustom, calls=%fused_computation.clone | custom fusion | bytes 286720 | tf_op jit(solution)/shard_map/jit(take_along_axis)/gather | solution.py:76
  162.7 1.5 copy.76
  164.7 78.2 %psum.127 = f32[16,384]{1,0:T(8,128)S(1)} all-reduce(f32[16,384]{1,0:T(8,128)S(1)} %convolution_bitcast_fusion.11), channel_id=1, replica_groups=mesh['gx'=32,'gy'=16] {'gy'}, use_global_device_ids=true, to_apply=%region_2.0 | all-reduce | flops 6144 | bytes 49152 | tf_op jit(solution)/shard_map/psum | solution.py:80
  244.1 1.8 fusion.5
  247.3 31.7 %gather_fusion.1 = f32[2048,16]{1,0:T(8,128)} fusion(f32[16,2,4,256]{0,3,2,1:T(8,128)} %copy.77, s32[2048]{0:T(1024)S(1)} %bitcast.281), kind=kCustom, calls=%fused_computation.1.clone | custom fusion | bytes 286720 | tf_op jit(solution)/shard_map/jit(take_along_axis)/gather | solution.py:84
  279.0 1.5 copy.78
  282.0 10.1 collective-permute-start.3
  293.5 107.1 %psum.128 = f32[16]{0:T(128)S(1)} all-reduce(f32[16]{0:T(128)S(1)} %multiply_reduce_fusion.5), channel_id=1, replica_groups=mesh['gx'=32,'gy'=16] {'gx','gy'}, use_global_device_ids=true, to_apply=%region_5.7 | all-reduce | flops 16 | bytes 128 | tf_op jit(solution)/shard_map/psum | solution.py:24
  400.8 94.4 %psum.129 = f32[16]{0:T(128)S(1)} all-reduce(f32[16]{0:T(128)S(1)} %get-tuple-element.23), channel_id=1, replica_groups=mesh['gx'=32,'gy'=16] {'gx','gy'}, use_global_device_ids=true, to_apply=%region_7.9 | all-reduce | flops 16 | bytes 128 | tf_op jit(solution)/shard_map/psum | solution.py:24
  495.6 4.2 collective-permute-start.5
  500.0 2.5 collective-permute-start.4
  505.0 31.7 %gather_fusion.2 = f32[2048,16]{1,0:T(8,128)} fusion(f32[16,2,4,256]{0,3,2,1:T(8,128)} %copy.89, s32[2048]{0:T(1024)S(1)} %bitcast.288), kind=kCustom, calls=%fused_computation.2.clone | custom fusion | bytes 286720 | tf_op jit(solution)/shard_map/jit(take_along_axis)/gather | solution.py:76
  538.6 78.2 %psum.130 = f32[16,384]{1,0:T(8,128)S(1)} all-reduce(f32[16,384]{1,0:T(8,128)S(1)} %convolution_bitcast_fusion.10), channel_id=1, replica_groups=mesh['gx'=32,'gy'=16] {'gy'}, use_global_device_ids=true, to_apply=%region_8.10 | all-reduce | flops 6144 | bytes 49152 | tf_op jit(solution)/shard_map/psum | solution.py:80
  618.1 1.8 fusion.4
  621.3 31.7 %gather_fusion.3 = f32[2048,16]{1,0:T(8,128)} fusion(f32[16,2,4,256]{0,3,2,1:T(8,128)} %copy.91, s32[2048]{0:T(1024)S(1)} %bitcast.282), kind=kCustom, calls=%fused_computation.3.clone | custom fusion | bytes 286720 | tf_op jit(solution)/shard_map/jit(take_along_axis)/gather | solution.py:84
  653.0 1.5 copy.92
  656.0 10.1 collective-permute-start.7
  667.5 106.2 %psum.131 = f32[16]{0:T(128)S(1)} all-reduce(f32[16]{0:T(128)S(1)} %multiply_reduce_fusion.4), channel_id=1, replica_groups=mesh['gx'=32,'gy'=16] {'gx','gy'}, use_global_device_ids=true, to_apply=%region_10.12 | all-reduce | flops 16 | bytes 128 | tf_op jit(solution)/shard_map/psum | solution.py:24
  773.9 94.4 %psum.132 = f32[16]{0:T(128)S(1)} all-reduce(f32[16]{0:T(128)S(1)} %get-tuple-element.21), channel_id=1, replica_groups=mesh['gx'=32,'gy'=16] {'gx','gy'}, use_global_device_ids=true, to_apply=%region_12.14 | all-reduce | flops 16 | bytes 128 | tf_op jit(solution)/shard_map/psum | solution.py:24
  868.6 4.2 collective-permute-start.9
  873.1 2.1 collective-permute-start.8
  877.6 31.7 %gather_fusion.4 = f32[2048,16]{1,0:T(8,128)} fusion(f32[16,2,4,256]{0,3,2,1:T(8,128)} %copy.101, s32[2048]{0:T(1024)S(1)} %bitcast.289), kind=kCustom, calls=%fused_computation.4.clone | custom fusion | bytes 286720 | tf_op jit(solution)/shard_map/jit(take_along_axis)/gather | solution.py:76
  909.3 1.5 copy.102
  911.3 78.2 %psum.133 = f32[16,384]{1,0:T(8,128)S(1)} all-reduce(f32[16,384]{1,0:T(8,128)S(1)} %convolution_bitcast_fusion.9), channel_id=1, replica_groups=mesh['gx'=32,'gy'=16] {'gy'}, use_global_device_ids=true, to_apply=%region_13.15 | all-reduce | flops 6144 | bytes 49152 | tf_op jit(solution)/shard_map/psum | solution.py:80
  990.8 1.8 fusion.3
  993.9 31.7 %gather_fusion.5 = f32[2048,16]{1,0:T(8,128)} fusion(f32[16,2,4,256]{0,3,2,1:T(8,128)} %copy.103, s32[2048]{0:T(1024)S(1)} %bitcast.283), kind=kCustom, calls=%fused_computation.5.clone | custom fusion | bytes 286720 | tf_op jit(solution)/shard_map/jit(take_along_axis)/gather | solution.py:84
  1028.7 10.1 collective-permute-start.11
  1040.1 106.4 %psum.134 = f32[16]{0:T(128)S(1)} all-reduce(f32[16]{0:T(128)S(1)} %multiply_reduce_fusion.3), channel_id=1, replica_groups=mesh['gx'=32,'gy'=16] {'gx','gy'}, use_global_device_ids=true, to_apply=%region_15.17 | all-reduce | flops 16 | bytes 128 | tf_op jit(solution)/shard_map/psum | solution.py:24
  1146.8 93.6 %psum.135 = f32[16]{0:T(128)S(1)} all-reduce(f32[16]{0:T(128)S(1)} %get-tuple-element.19), channel_id=1, replica_groups=mesh['gx'=32,'gy'=16] {'gx','gy'}, use_global_device_ids=true, to_apply=%region_17.19 | all-reduce | flops 16 | bytes 128 | tf_op jit(solution)/shard_map/psum | solution.py:24
  1241.3 4.2 collective-permute-start.13
  1245.8 2.9 collective-permute-start.12
  1251.9 31.7 %gather_fusion.6 = f32[2048,16]{1,0:T(8,128)} fusion(f32[16,2,4,256]{0,3,2,1:T(8,128)} %copy.113, s32[2048]{0:T(1024)S(1)} %bitcast.290), kind=kCustom, calls=%fused_computation.6.clone | custom fusion | bytes 286720 | tf_op jit(solution)/shard_map/jit(take_along_axis)/gather | solution.py:76
  1283.6 1.5 copy.114
  1285.6 78.0 %psum.136 = f32[16,384]{1,0:T(8,128)S(1)} all-reduce(f32[16,384]{1,0:T(8,128)S(1)} %convolution_bitcast_fusion.8), channel_id=1, replica_groups=mesh['gx'=32,'gy'=16] {'gy'}, use_global_device_ids=true, to_apply=%region_18.20 | all-reduce | flops 6144 | bytes 49152 | tf_op jit(solution)/shard_map/psum | solution.py:80
  1364.8 1.8 fusion.2
  1368.0 31.7 %gather_fusion.7 = f32[2048,16]{1,0:T(8,128)} fusion(f32[16,2,4,256]{0,3,2,1:T(8,128)} %copy.115, s32[2048]{0:T(1024)S(1)} %bitcast.284), kind=kCustom, calls=%fused_computation.7.clone | custom fusion | bytes 286720 | tf_op jit(solution)/shard_map/jit(take_along_axis)/gather | solution.py:84
  1402.7 10.1 collective-permute-start.15
  1414.2 106.2 %psum.137 = f32[16]{0:T(128)S(1)} all-reduce(f32[16]{0:T(128)S(1)} %multiply_reduce_fusion.2), channel_id=1, replica_groups=mesh['gx'=32,'gy'=16] {'gx','gy'}, use_global_device_ids=true, to_apply=%region_20.22 | all-reduce | flops 16 | bytes 128 | tf_op jit(solution)/shard_map/psum | solution.py:24
  1520.6 94.4 %psum.138 = f32[16]{0:T(128)S(1)} all-reduce(f32[16]{0:T(128)S(1)} %get-tuple-element.17), channel_id=1, replica_groups=mesh['gx'=32,'gy'=16] {'gx','gy'}, use_global_device_ids=true, to_apply=%region_22.24 | all-reduce | flops 16 | bytes 128 | tf_op jit(solution)/shard_map/psum | solution.py:24
  1616.0 4.2 collective-permute-start.17
  1620.4 2.1 collective-permute-start.16
  1625.8 31.7 %gather_fusion.8 = f32[2048,16]{1,0:T(8,128)} fusion(f32[16,2,4,256]{0,3,2,1:T(8,128)} %copy.125, s32[2048]{0:T(1024)S(1)} %bitcast.291), kind=kCustom, calls=%fused_computation.8.clone | custom fusion | bytes 286720 | tf_op jit(solution)/shard_map/jit(take_along_axis)/gather | solution.py:76
  1657.5 1.5 copy.126
  1659.5 78.6 %psum.139 = f32[16,384]{1,0:T(8,128)S(1)} all-reduce(f32[16,384]{1,0:T(8,128)S(1)} %convolution_bitcast_fusion.7), channel_id=1, replica_groups=mesh['gx'=32,'gy'=16] {'gy'}, use_global_device_ids=true, to_apply=%region_23.25 | all-reduce | flops 6144 | bytes 49152 | tf_op jit(solution)/shard_map/psum | solution.py:80
  1739.3 2.5 fusion.1
  1741.8 2.2 copy.127
  1744.1 31.7 %gather_fusion.9 = f32[2048,16]{1,0:T(8,128)} fusion(f32[16,2,4,256]{0,3,2,1:T(8,128)} %copy.127, s32[2048]{0:T(1024)S(1)} %bitcast.285), kind=kCustom, calls=%fused_computation.9.clone | custom fusion | bytes 286720 | tf_op jit(solution)/shard_map/jit(take_along_axis)/gather | solution.py:84
  1775.7 2.2 copy.128
  1780.3 10.1 collective-permute-start.19
  1791.8 106.2 %psum.140 = f32[16]{0:T(128)S(1)} all-reduce(f32[16]{0:T(128)S(1)} %multiply_reduce_fusion.1), channel_id=1, replica_groups=mesh['gx'=32,'gy'=16] {'gx','gy'}, use_global_device_ids=true, to_apply=%region_25.27 | all-reduce | flops 16 | bytes 128 | tf_op jit(solution)/shard_map/psum | solution.py:24
  1899.1 93.6 %psum.141 = f32[16]{0:T(128)S(1)} all-reduce(f32[16]{0:T(128)S(1)} %get-tuple-element.15), channel_id=1, replica_groups=mesh['gx'=32,'gy'=16] {'gx','gy'}, use_global_device_ids=true, to_apply=%region_27.29 | all-reduce | flops 16 | bytes 128 | tf_op jit(solution)/shard_map/psum | solution.py:24
  1993.6 4.2 collective-permute-start.21
  1998.1 2.9 collective-permute-start.20
  2004.3 31.7 %gather_fusion.10 = f32[2048,16]{1,0:T(8,128)} fusion(f32[16,2,4,256]{0,3,2,1:T(8,128)} %copy.137, s32[2048]{0:T(1024)S(1)} %bitcast.292), kind=kCustom, calls=%fused_computation.10.clone | custom fusion | bytes 286720 | tf_op jit(solution)/shard_map/jit(take_along_axis)/gather | solution.py:76
  2036.0 1.5 copy.138
  2038.0 78.0 %psum.142 = f32[16,384]{1,0:T(8,128)S(1)} all-reduce(f32[16,384]{1,0:T(8,128)S(1)} %convolution_bitcast_fusion.6), channel_id=1, replica_groups=mesh['gx'=32,'gy'=16] {'gy'}, use_global_device_ids=true, to_apply=%region_28.30 | all-reduce | flops 6144 | bytes 49152 | tf_op jit(solution)/shard_map/psum | solution.py:80
  2117.2 1.8 fusion
  2120.4 31.7 %gather_fusion.11 = f32[2048,16]{1,0:T(8,128)} fusion(f32[16,2,4,256]{0,3,2,1:T(8,128)} %copy.139, s32[2048]{0:T(1024)S(1)} %bitcast.286), kind=kCustom, calls=%fused_computation.11.clone | custom fusion | bytes 286720 | tf_op jit(solution)/shard_map/jit(take_along_axis)/gather | solution.py:84
  2155.1 10.1 collective-permute-start.23
  2167.2 106.2 %psum.143 = f32[16]{0:T(128)S(1)} all-reduce(f32[16]{0:T(128)S(1)} %multiply_reduce_fusion), channel_id=1, replica_groups=mesh['gx'=32,'gy'=16] {'gx','gy'}, use_global_device_ids=true, to_apply=%region_30.32 | all-reduce | flops 16 | bytes 128 | tf_op jit(solution)/shard_map/psum | solution.py:24
  (326 shorter events, 72.9 us)
Async XLA Ops:
  7.2 237.0 %copy-start = (f32[2,4,256,256]{3,2,1,0:T(8,128)S(1)}, f32[2,4,256,256]{3,2,1,0:T(8,128)}, u32[]{:S(2)}) copy-start(f32[2,4,256,256]{3,2,1,0:T(8,128)} %param.17) | copy-start | bytes 6291460
  7.2 120.7 %sort.19.cloned.1.call-start = ((), (), s32[]{:S(2)}) async-start(), calls=%async_computation | async-start | bytes 49184 | tf_op jit(solution)/shard_map/jit(argsort)/sort | solution.py:53
  117.1 12.3 collective-permute-start
  119.1 10.2 collective-permute-start.1
  129.6 34.6 %copy-start.2 = (f32[2,4,8,256]{3,2,1,0:T(8,128)S(1)}, f32[2,4,8,256]{3,2,1,0:T(8,128)}, u32[]{:S(2)}) copy-start(f32[2,4,8,256]{3,2,1,0:T(8,128)} %param.18) | copy-start | bytes 196612
  131.0 33.5 %copy-start.12 = (s32[2,4,8]{2,1,0:T(4,128)S(1)}, s32[2,4,8]{2,1,0:T(4,128)}, u32[]{:S(2)}) copy-start(s32[2,4,8]{2,1,0:T(4,128)} %param.21) | copy-start | bytes 772
  131.0 111.9 %copy-start.1 = (f32[1,384,384]{2,1,0:T(8,128)S(1)}, f32[1,384,384]{2,1,0:T(8,128)}, u32[]{:S(2)}) copy-start(f32[1,384,384]{2,1,0:T(8,128)} %param.19) | copy-start | bytes 1769476
  247.3 153.3 %copy-start.3 = (f32[16,2,4,128]{3,2,1,0:T(4,128)S(1)}, f32[16,2,4,128]{3,2,1,0:T(4,128)}, u32[]{:S(2)}) copy-start(f32[16,2,4,128]{3,2,1,0:T(4,128)} %param.14) | copy-start | bytes 196612
  280.6 12.4 collective-permute-start.2
  282.0 11.0 collective-permute-start.3
  495.6 7.0 collective-permute-start.5
  500.0 3.4 collective-permute-start.4
  654.6 12.4 collective-permute-start.6
  656.0 10.9 collective-permute-start.7
  773.7 135.6 %copy-start.6 = (f32[16]{0:T(128)}, f32[16]{0:T(128)S(1)}, u32[]{:S(2)}) copy-start(f32[16]{0:T(128)S(1)} %div.39) | copy-start | bytes 196
  868.6 6.6 collective-permute-start.9
  873.1 3.0 collective-permute-start.8
  1027.3 12.4 collective-permute-start.10
  1028.7 10.9 collective-permute-start.11
  1146.5 137.1 %copy-start.8 = (f32[16]{0:T(128)}, f32[16]{0:T(128)S(1)}, u32[]{:S(2)}) copy-start(f32[16]{0:T(128)S(1)} %div.41) | copy-start | bytes 196
  1241.3 7.3 collective-permute-start.13
  1245.8 3.8 collective-permute-start.12
  1401.3 12.4 collective-permute-start.14
  1402.7 10.9 collective-permute-start.15
  1520.4 137.1 %copy-start.10 = (f32[16]{0:T(128)}, f32[16]{0:T(128)S(1)}, u32[]{:S(2)}) copy-start(f32[16]{0:T(128)S(1)} %div.43) | copy-start | bytes 196
  1615.0 42.5 %copy-start.14 = (f32[16]{0:T(128)}, f32[16]{0:T(128)S(1)}, u32[]{:S(2)}) copy-start(f32[16]{0:T(128)S(1)} %psum.138) | copy-start | bytes 196
  1616.0 6.6 collective-permute-start.17
  1620.4 3.0 collective-permute-start.16
  1744.1 153.9 %copy-start.15 = (f32[16]{0:T(128)S(1)}, f32[16]{0:T(128)}, u32[]{:S(2)}) copy-start(f32[16]{0:T(128)} %copy-done.14) | copy-start | bytes 196
  1778.9 12.4 collective-permute-start.18
  1780.3 10.9 collective-permute-start.19
  1791.6 106.4 %copy-start.4 = (f32[16,2,4,64]{3,0,2,1:T(8,128)}, f32[16,2,4,64]{3,0,2,1:T(8,128)S(1)}, u32[]{:S(2)}) copy-start(f32[16,2,4,64]{3,0,2,1:T(8,128)S(1)} %get-tuple-element.30) | copy-start | bytes 98308
  1992.7 43.3 %copy-start.16 = (f32[16]{0:T(128)}, f32[16]{0:T(128)S(1)}, u32[]{:S(2)}) copy-start(f32[16]{0:T(128)S(1)} %psum.141) | copy-start | bytes 196
  1993.6 7.4 collective-permute-start.21
  1998.1 3.8 collective-permute-start.20
  2004.3 33.5 %copy-start.13 = (s32[2,4,8]{2,1,0:T(4,128)S(1)}, s32[2,4,8]{2,1,0:T(4,128)}, u32[]{:S(2)}) copy-start(s32[2,4,8]{2,1,0:T(4,128)} %param.21) | copy-start | bytes 772
  2120.4 153.0 %copy-start.17 = (f32[16]{0:T(128)S(1)}, f32[16]{0:T(128)}, u32[]{:S(2)}) copy-start(f32[16]{0:T(128)} %copy-done.16) | copy-start | bytes 196
  2120.4 153.0 %copy-start.5 = (f32[16,2,4,128]{3,2,1,0:T(4,128)S(1)}, f32[16,2,4,128]{3,2,1,0:T(4,128)}, u32[]{:S(2)}) copy-start(f32[16,2,4,128]{3,2,1,0:T(4,128)} %param.13) | copy-start | bytes 196612
  2120.4 153.0 %copy-start.7 = (f32[16]{0:T(128)S(1)}, f32[16]{0:T(128)}, u32[]{:S(2)}) copy-start(f32[16]{0:T(128)} %copy-done.6) | copy-start | bytes 196
  2120.4 153.0 %copy-start.9 = (f32[16]{0:T(128)S(1)}, f32[16]{0:T(128)}, u32[]{:S(2)}) copy-start(f32[16]{0:T(128)} %copy-done.8) | copy-start | bytes 196
  2120.4 153.0 %copy-start.11 = (f32[16]{0:T(128)S(1)}, f32[16]{0:T(128)}, u32[]{:S(2)}) copy-start(f32[16]{0:T(128)} %copy-done.10) | copy-start | bytes 196
  2153.7 12.4 collective-permute-start.22
  2155.1 10.9 collective-permute-start.23
Sparse Core Ops, SparseCore 0:
  123.1 4.4 sort.21.cloned.1.call-done
  (1 shorter events, 0.0 us)
where the time goes:
time: 2290 us; the launch traced here: 2280 us
  blocking collectives  1680 us (73%)
  local copies, waits for them, and re-layouts  430 us (19%)
  starting transfers between devices  107 us (5%)
    psum x12, blocking collectives, case_sum(): return lax.psum(values, ('gx', 'gy'))  1210 us
    psum x6, blocking collectives, shards(): total = lax.psum(partial_total, 'gy')  469 us
    gather x12, local copies, waits for them, and re-layouts, shards(): work_edge = jnp.take_along_axis(work, inverse[None], -1)  200 us
    gather x12, local copies, waits for them, and re-layouts, shards(): local = jnp.take_along_axis(edge_vec, edge_map[None], -1)  199 us
    ppermute x24, starting transfers between devices, passed_along(): return lax.ppermute(value, axis, pairs)  107 us
  transfers between devices with their start and end apart: 24, of which 11 were waited for; matrix products, arithmetic and copies ran while one was open for 0% of the time, Pallas kernels for 0%

commit v1 on v0

v1 whole, which is shorter than its diff:
```python
import functools

import jax
import jax.numpy as jnp
from jax import lax
from jax.experimental import pallas as pl
from jax.experimental.pallas import tpu as pltpu
from jax.sharding import PartitionSpec as P

MESH = pl.DeviceIdType.MESH
NT = (((1,), (1,)), ((), ()))
F32 = jnp.float32
BF16 = jnp.bfloat16


def dot(a, b):
    return jnp.dot(a, b, preferred_element_type=F32)


def dot_nt(a, b):
    return lax.dot_general(a, b, NT, preferred_element_type=F32)


def split(v):
    hi = v.astype(BF16)
    return hi, (v - hi.astype(F32)).astype(BF16)


def iota(shape, dim):
    return lax.broadcasted_iota(jnp.int32, shape, dim)


def remote(src, dst, send, recv, dev):
    return pltpu.make_async_remote_copy(
        src_ref=src, dst_ref=dst, send_sem=send, recv_sem=recv, device_id=dev, device_id_type=MESH
    )


class Group:
    def __init__(self, n, me, dev, src, dst, send, recv):
        self.n, self.me, self.dev, self.src, self.dst, self.send_sem, self.recv_sem = n, me, dev, src, dst, send, recv

    def each(self, fn):
        def body(j, c):
            fn(j)
            return c

        lax.fori_loop(1, self.n, body, 0, unroll=True)

    def copy_to(self, j):
        peer = lax.rem(self.me + j, self.n)
        return remote(self.src, self.dst.at[self.me], self.send_sem.at[j], self.recv_sem.at[self.me], self.dev(peer))

    def copy_from(self, j):
        peer = lax.rem(self.me + j, self.n)
        return remote(self.src, self.dst.at[peer], self.send_sem.at[j], self.recv_sem.at[peer], self.dev(peer))

    def start(self, value):
        self.src[...] = value
        self.dst[self.me] = value
        self.each(lambda j: self.copy_to(j).start())

    def wait(self):
        self.each(lambda j: self.copy_from(j).wait_recv())

    def finish(self):
        self.each(lambda j: self.copy_to(j).wait_send())


def kernel(
    gxn, gyn, zn, iters,
    duals, residual, direction, misc, schur, coupling, ainv, emap, active, scaling,
    out_l, out_r, out_p,
    s_hi, s_lo, g_hi, g_lo, m_hi, m_lo, lhs,
    lam, res, pv, qv, wv, tv, xv, keep, dv, wk, wn,
    h_w, h_s, r_e, r_n, g1, ct, d1, d2, d3, c1, c2, c3, sl, slsrc, sc,
    hsend, hrecv, gsend, grecv, d1s, d1r, d2s, d2r, d3s, d3r, sls, slr,
):
    gx = lax.axis_index("gx")
    gy = lax.axis_index("gy")
    yn = gxn // zn
    zpos, ypos = lax.rem(gx, zn), gx // zn
    has_w, has_e = gx > 0, gx < gxn - 1
    has_s, has_n = gy > 0, gy < gyn - 1
    by_y = lambda i: (gx, i)
    by_z = lambda i: (ypos * zn + i, gy)
    by_o = lambda i: (i * zn + zpos, gy)

    for ref in (h_w, h_s, r_e, r_n):
        ref[...] = jnp.zeros_like(ref)

    barrier = pltpu.get_barrier_semaphore()

    def greet(n, me, dev):
        def body(j, c):
            pl.semaphore_signal(barrier, inc=1, device_id=dev(lax.rem(me + j, n)), device_id_type=MESH)
            return c

        lax.fori_loop(1, n, body, 0, unroll=True)

    greet(gyn, gy, by_y)
    greet(zn, zpos, by_z)
    greet(yn, ypos, by_o)

    @pl.when(has_e)
    def _():
        pl.semaphore_signal(barrier, inc=1, device_id=(gx + 1, gy), device_id_type=MESH)

    @pl.when(has_w)
    def _():
        pl.semaphore_signal(barrier, inc=1, device_id=(gx - 1, gy), device_id_type=MESH)

    lane = iota((16, 128), 1)
    row = iota((16, 128), 0)
    low = lane < 64
    low8 = iota((8, 128), 1) < 64

    for a in range(2):
        for b in range(4):
            s = a * 4 + b
            lam[s] = duals[:, a, b, :]
            res[s] = residual[:, a, b, :]
            kp = jnp.broadcast_to(active[a, b : b + 1, :].astype(F32), (16, 128))
            if a == 1:
                kp = jnp.where(jnp.logical_or(has_e, lane >= 64), kp, 0.0)
            if b == 3:
                kp = jnp.where(jnp.logical_or(has_n, lane < 64), kp, 0.0)
            keep[s] = kp
            dv[s] = kp * jnp.broadcast_to(scaling[a, b : b + 1, :], (16, 128))
            pv[s] = kp * direction[:, a, b, :]

    def dots(pairs):
        acc = jnp.zeros((16, 128), F32)
        for d, prod in enumerate(pairs):
            col = jnp.sum(jnp.sum(prod, axis=0), axis=1, keepdims=True)
            acc = jnp.where(lane == row + 16 * d, jnp.broadcast_to(col, (16, 128)), acc)
        return jnp.sum(acc, axis=0, keepdims=True)

    def column(line, d):
        picked = jnp.where(lane == row + 16 * d, jnp.broadcast_to(line, (16, 128)), 0.0)
        return jnp.broadcast_to(jnp.sum(picked, axis=1, keepdims=True), (16, 128))

    def stages(par):
        return (
            Group(gyn, gy, by_y, c1, d1.at[par], d1s, d1r.at[par]),
            Group(zn, zpos, by_z, c2, d2.at[par], d2s, d2r.at[par]),
            Group(yn, ypos, by_o, c3, d3.at[par], d3s, d3r.at[par]),
        )

    def total(group):
        group.wait()
        return jnp.sum(group.dst[...], axis=0)

    slots = Group(gyn, gy, by_y, slsrc, sl, sls, slr)
    first = stages(0)
    rho_line = dots([res[...] * (dv[...] * res[...])])

    pl.semaphore_wait(
        barrier, (gyn - 1) + (zn - 1) + (yn - 1) + has_e.astype(jnp.int32) + has_w.astype(jnp.int32)
    )
    first[0].start(rho_line)
    slots.start(misc[0])

    e = iota((256, 256), 0)
    orig = jnp.where(e < 64, e + 64, jnp.where(e < 128, e + 128, jnp.where(e < 192, e - 128, e - 64)))
    sign = jnp.where(e < 128, 1.0, -1.0)
    grow = iota((128, 256), 0)
    for a in range(2):
        for b in range(4):
            s = a * 4 + b
            em = jnp.broadcast_to(emap[a, b : b + 1, :], (256, 256))
            pt = jnp.where(em == orig, sign, 0.0).astype(BF16)
            sh, slo = split(schur[s])
            s_hi[s] = dot(pt, dot_nt(sh, pt).astype(BF16)).astype(BF16)
            s_lo[s] = dot(pt, dot_nt(slo, pt).astype(BF16)).astype(BF16)
            ch, cl = split(coupling[s])
            here = (grow % 64) // 8 == s
            for part, ref in ((ch, g_hi), (cl, g_lo)):
                turned = dot_nt(part, pt)
                ref[s] = jnp.where(here, jnp.concatenate([turned] * 16, axis=0), 0.0).astype(BF16)
        if a == 0:
            first[1].start(total(first[0]))
    first[2].start(total(first[1]))

    width = ainv.shape[0]
    slots.wait()
    own = jnp.transpose(jnp.broadcast_to(misc[0], (128, 128)))
    own_hot = jnp.where(
        jnp.concatenate([own] * (width // 128), axis=1) == iota((128, width), 1).astype(F32), 1.0, 0.0
    ).astype(BF16)
    ah, al = split(ainv[...])
    yh, yl = dot(own_hot, ah).astype(BF16), dot(own_hot, al).astype(BF16)
    tall = iota((width, 128), 0).astype(F32)
    for pair in range(gyn // 2):
        both = jnp.where(low8[:1], sl[2 * pair], pltpu.roll(sl[2 * pair + 1], 64, 1))
        hot = jnp.where(tall == jnp.broadcast_to(both, (width, 128)), 1.0, 0.0).astype(BF16)
        cols = slice(pair * 128, pair * 128 + 128)
        m_hi[:, cols] = dot(yh, hot).astype(BF16)
        m_lo[:, cols] = dot(yl, hot).astype(BF16)

    line = total(first[2])
    rho = column(line, 0)
    beta = rho / column(misc[1], 0)
    pv[...] = dv[...] * res[...] + beta * pv[...]
    xv[...] = pv[...].reshape(2, 4, 16, 128)
    sc[0] = rho
    sc[1] = rho
    for group in first:
        group.finish()
    slots.finish()

    def halo(par):
        return (
            remote(xv.at[1], h_w.at[par], hsend.at[0], hrecv.at[par, 0], (gx + 1, gy)),
            remote(xv.at[:, 3], h_s.at[par], hsend.at[1], hrecv.at[par, 1], (gx, gy + 1)),
            remote(wn.at[0], r_e.at[par], hsend.at[2], hrecv.at[par, 2], (gx - 1, gy)),
            remote(wn.at[:, 0], r_n.at[par], hsend.at[3], hrecv.at[par, 3], (gx, gy - 1)),
        )

    sends = (has_e, has_n, has_w, has_s)
    receives = (has_w, has_s, has_e, has_n)

    def each_of(copies, which, go, verb):
        for i in which:
            pl.when(go[i])(lambda i=i: getattr(copies[i], verb)())

    def fold(v):
        return v[:16] + v[16:]

    def apply(par, line):
        copies = halo(par)
        reduce_y, reduce_z, reduce_o = stages(par)
        coarse = Group(gyn, gy, by_y, ct, g1.at[par], gsend, grecv.at[par])
        each_of(copies, (0, 1), sends, "start")
        reduce_y.start(line)
        each_of(copies, (0, 1), receives, "wait_recv")
        v2 = jnp.zeros((16, 128), F32)
        for a in range(2):
            for b in range(4):
                s = a * 4 + b
                west = h_w[par, b] if a == 0 else xv[0, b]
                south = h_s[par, a] if b == 0 else xv[a, b - 1]
                hi, lo = split(jnp.concatenate([xv[a, b], jnp.where(low, west, south)], axis=1))
                lhs[s, :16] = hi
                lhs[s, 16:] = lo
                v2 = v2 + fold(dot_nt(jnp.concatenate([hi, lo], axis=0), g_hi[s])) + dot_nt(hi, g_lo[s])
        coarse.start(jnp.where(low8, v2[:8], v2[8:]))
        reduce_z.start(total(reduce_y))
        for s in range(8):
            wk[s] = fold(dot(lhs[s], s_hi[s])) + dot(lhs[s, :16], s_lo[s])
        coarse.wait()
        pieces = []
        for pair in range(gyn // 2):
            one, two = g1[par, 2 * pair], g1[par, 2 * pair + 1]
            top = jnp.where(low8, one, pltpu.roll(two, 64, 1))
            bottom = jnp.where(low8, pltpu.roll(one, 64, 1), two)
            pieces.append(jnp.concatenate([top, bottom], axis=0))
        hi, lo = split(jnp.concatenate(pieces, axis=1))
        back = fold(dot_nt(jnp.concatenate([hi, lo], axis=0), m_hi[...])) + dot_nt(hi, m_lo[...])
        bhi, blo = split(back)
        bhl = jnp.concatenate([bhi, blo], axis=0)
        for s in range(8):
            full = wk[s] + fold(dot(bhl, g_hi[s])) + dot(bhi, g_lo[s])
            wk[s] = full
            wn[s // 4, s % 4] = full[:, 128:]
        each_of(copies, (2, 3), sends, "start")
        reduce_o.start(total(reduce_z))
        summed = total(reduce_o)
        each_of(copies, (2, 3), receives, "wait_recv")
        result = []
        for a in range(2):
            for b in range(4):
                east = r_e[par, b] if a == 1 else wn[1, b]
                north = r_n[par, a] if b == 3 else wn[a, b + 1]
                result.append(wk[a * 4 + b, :, :128] + jnp.where(low, east, north))
        each_of(copies, (0, 1, 2, 3), sends, "wait_send")
        for group in (reduce_y, reduce_z, reduce_o, coarse):
            group.finish()
        return jnp.stack(result) * keep[...], summed

    def residual_dots():
        z = dv[...] * res[...]
        return dots([res[...] * z, z * wv[...], z * qv[...]])

    def step_of(line):
        rho = column(line, 0)
        beta = rho / sc[0]
        pq = column(line, 1) + beta * (2.0 * column(line, 2) + beta * sc[1])
        alpha = rho / pq
        sc[0] = rho
        sc[1] = pq
        return beta, alpha, dv[...] * res[...] + beta * pv[...]

    def round_body(i, line):
        got, summed = apply(lax.rem(i + 1, 2), line)
        nxt = c1

        @pl.when(i == 0)
        def _():
            qv[...] = got
            xv[...] = (dv[...] * got).reshape(2, 4, 16, 128)
            nxt[...] = dots([pv[...] * got])

        @pl.when(i == 1)
        def _():
            tv[...] = got
            pq = column(summed, 0)
            alpha = sc[0] / pq
            sc[1] = pq
            lam[...] += alpha * pv[...]
            new = res[...] - alpha * qv[...]
            res[...] = new
            xv[...] = (dv[...] * new).reshape(2, 4, 16, 128)

        @pl.when(i == 2)
        def _():
            wv[...] = got
            xv[...] = (dv[...] * got).reshape(2, 4, 16, 128)
            nxt[...] = residual_dots()

        @pl.when(i >= 3)
        def _():
            beta, alpha, p = step_of(summed)
            pv[...] = p
            q = wv[...] + beta * qv[...]
            t = got + beta * tv[...]
            qv[...] = q
            tv[...] = t
            lam[...] += alpha * p
            res[...] -= alpha * q
            w = wv[...] - alpha * t
            wv[...] = w
            xv[...] = (dv[...] * w).reshape(2, 4, 16, 128)
            nxt[...] = residual_dots()

        return nxt[...]

    rounds = iters + 1
    line = lax.fori_loop(0, rounds, round_body, rho_line)

    last = stages((rounds + 1) % 2)
    last[0].start(line)
    last[1].start(total(last[0]))
    last[2].start(total(last[1]))
    beta, alpha, p = step_of(total(last[2]))
    new_l = lam[...] + alpha * p
    new_r = res[...] - alpha * (wv[...] + beta * qv[...])
    for a in range(2):
        for b in range(4):
            s = a * 4 + b
            out_l[:, a, b, :] = new_l[s]
            out_r[:, a, b, :] = new_r[s]
            out_p[:, a, b, :] = p[s]
    for group in last:
        group.finish()


def shards(gxn, gyn, zn, duals, residual, direction, prev_rho, schur, coupling, ainv, emap, slot, active, scaling):
    misc = jnp.stack([
        jnp.pad(slot.reshape(1, 64).astype(F32), ((0, 0), (0, 64)), constant_values=float(ainv.shape[-1])),
        jnp.pad(prev_rho.reshape(1, 16), ((0, 0), (0, 112))),
    ])
    yn = gxn // zn
    vmem = pl.BlockSpec(memory_space=pltpu.VMEM)
    field = jax.ShapeDtypeStruct(duals.shape, F32)
    tiles = lambda *lead: pltpu.VMEM(lead + (16, 128), F32)
    line = lambda *lead: pltpu.VMEM(lead + (1, 128), F32)
    dma = lambda *shape: pltpu.SemaphoreType.DMA(shape)
    return pl.pallas_call(
        functools.partial(kernel, gxn, gyn, zn, 6),
        out_shape=(field, field, field),
        in_specs=[vmem] * 10,
        out_specs=(vmem, vmem, vmem),
        scratch_shapes=[
            pltpu.VMEM((8, 256, 256), BF16), pltpu.VMEM((8, 256, 256), BF16),
            pltpu.VMEM((8, 128, 256), BF16), pltpu.VMEM((8, 128, 256), BF16),
            pltpu.VMEM((128, 64 * gyn), BF16), pltpu.VMEM((128, 64 * gyn), BF16),
            pltpu.VMEM((8, 32, 256), BF16),
            tiles(8), tiles(8), tiles(8), tiles(8), tiles(8), tiles(8), tiles(2, 4), tiles(8), tiles(8),
            pltpu.VMEM((8, 16, 256), F32), tiles(2, 4),
            tiles(2, 4), tiles(2, 2), tiles(2, 4), tiles(2, 2),
            pltpu.VMEM((2, gyn, 8, 128), F32), pltpu.VMEM((8, 128), F32),
            line(2, gyn), line(2, zn), line(2, yn), line(), line(), line(),
            line(gyn), line(), tiles(2),
            dma(4), dma(2, 4), dma(gyn), dma(2, gyn),
            dma(gyn), dma(2, gyn), dma(zn), dma(2, zn), dma(yn), dma(2, yn), dma(gyn), dma(gyn),
        ],
        compiler_params=pltpu.CompilerParams(collective_id=0, has_side_effects=True),
    )(duals, residual, direction, misc, schur.reshape(8, 256, 256), coupling.reshape(8, 8, 256), ainv[0], emap, active, scaling)


def solution(mesh):
    gxn, gyn = mesh.shape["gx"], mesh.shape["gy"]
    zn = 8 if gxn % 8 == 0 else 2
    grid = P(None, "gx", "gy", None)
    cells = P("gx", "gy", None)
    return jax.shard_map(
        functools.partial(shards, gxn, gyn, zn),
        mesh=mesh,
        in_specs=(
            grid, grid, grid, P(), P("gx", "gy", None, None), P("gx", "gy", None, None), P("gx", None, None),
            cells, cells, cells, cells,
        ),
        out_specs=(grid, grid, grid),
        check_vma=False,
    )
```

time: 2290 us -> 169 us (0.07)
  blocking collectives: 1680 us -> 0 us
  local copies, waits for them, and re-layouts: 430 us -> 5.17 us
  Pallas kernels: 0 us -> 161 us
  starting transfers between devices: 107 us -> 0 us
    psum x18 -> x0, blocking collectives: 1680 us -> none  [the longest x12 1210 us: case_sum(): return lax.psum(values, ('gx', 'gy'))]
    gather x24 -> x0, local copies, waits for them, and re-layouts: 399 us -> none  [the longest x12 200 us: shards(): work_edge = jnp.take_along_axis(work, inverse[None], -1)]
    pallas_call x0 -> x1, Pallas kernels: none -> 161 us  [shards(): pl.pallas_call(functools.partial(kernel, gxn, gyn, zn, 6), out_shape=(fie...]
    ppermute x24 -> x0, starting transfers between devices: 107 us -> none  [passed_along(): return lax.ppermute(value, axis, pairs)]
  transfers between devices with their start and end apart: 24 -> 0, of which waited for: 11 -> 0; matrix products, arithmetic and copies ran while one was open for 0% -> 0% of each run, Pallas kernels for 0% -> 0%
where the time goes in v1:
time: 169 us; the launch traced here: 168 us
  Pallas kernels  161 us (95%)
  local copies, waits for them, and re-layouts  5.17 us (3%)
    pallas_call x1, Pallas kernels, shards(): pl.pallas_call(functools.partial(kernel, gxn, gyn, zn, 6), out_shape=(fie...  161 us
    unnamed x3, local copies, waits for them, and re-layouts  4.42 us

profile of v1, /device:TPU:1, one launch (start us, length us, event | category | flops | bytes accessed | tf_op | source)
XLA Modules:
  0.0 168.1 jit_solution(14264932673581406033)
XLA Ops:
  0.6 0.7 convert_element_type.16
  1.3 0.1 convert_element_type.17
  1.4 0.7 pad_bitcast_fusion
  2.1 0.6 pad_maximum_fusion.misc
  2.6 161.1 %shard_map.130 = (f32[16,2,4,128]{3,2,1,0:T(4,128)}, f32[16,2,4,128]{3,2,1,0:T(4,128)}, f32[16,2,4,128]{3,2,1,0:T(4,128)}) custom-call(f32[16,2,4,128]{3,2,1,0:T(4,128)} %duals.1, f32[16,2,4,128]{3,2,1,0:T(4,128)} %residual.1, f32[16,2,4,128]{3,2,1,0:T(4,128)} %direction.1, f32[2,1,128]{2,1,0:T(1,128)} %pad_maximum_fusion.misc, f32[8,256,256]{2,1,0:T(8,128)} %bitcast.8, ...), custom_call_target="tpu_custom_call" | custom-call | tf_op jit(solution)/shard_map/pallas_call | solution.py:369
  163.7 1.5 copy.17
  165.2 1.5 copy.18
  166.7 1.5 copy.19

commit v2 on v1

v2 whole, which is shorter than its diff:
```python
import functools

import jax
import jax.numpy as jnp
from jax import lax
from jax.experimental import pallas as pl
from jax.experimental.pallas import tpu as pltpu
from jax.sharding import PartitionSpec as P

MESH = pl.DeviceIdType.MESH
NT = (((1,), (1,)), ((), ()))
F32 = jnp.float32
BF16 = jnp.bfloat16


def dot(a, b):
    return jnp.dot(a, b, preferred_element_type=F32)


def dot_nt(a, b):
    return lax.dot_general(a, b, NT, preferred_element_type=F32)


def split(v):
    hi = v.astype(BF16)
    return hi, (v - hi.astype(F32)).astype(BF16)


def iota(shape, dim):
    return lax.broadcasted_iota(jnp.int32, shape, dim)


def remote(src, dst, send, recv, dev):
    return pltpu.make_async_remote_copy(
        src_ref=src, dst_ref=dst, send_sem=send, recv_sem=recv, device_id=dev, device_id_type=MESH
    )


class Group:
    def __init__(self, n, me, dev, src, dst, send, recv):
        self.n, self.me, self.dev, self.src, self.dst, self.send_sem, self.recv_sem = n, me, dev, src, dst, send, recv

    def each(self, fn):
        def body(j, c):
            fn(j)
            return c

        lax.fori_loop(1, self.n, body, 0, unroll=True)

    def copy_to(self, j):
        peer = lax.rem(self.me + j, self.n)
        return remote(self.src, self.dst.at[self.me], self.send_sem.at[j], self.recv_sem.at[self.me], self.dev(peer))

    def copy_from(self, j):
        peer = lax.rem(self.me + j, self.n)
        return remote(self.src, self.dst.at[peer], self.send_sem.at[j], self.recv_sem.at[peer], self.dev(peer))

    def start(self, value):
        self.src[...] = value
        self.dst[self.me] = value
        self.each(lambda j: self.copy_to(j).start())

    def wait(self):
        self.each(lambda j: self.copy_from(j).wait_recv())

    def finish(self):
        self.each(lambda j: self.copy_to(j).wait_send())


def kernel(
    gxn, gyn, zn, yhn, iters,
    duals, residual, direction, prev_rho, schur, coupling, ainv, emap, slot, active, scaling,
    out_l, out_r, out_p,
    s_hi, s_lo, g_hi, g_lo, m_hi, m_lo, lhs,
    lam, res, pv, qv, wv, tv, xv, keep, dv, wk, wn,
    h_w, h_s, r_e, h_n, h_nw, g1, ct, d1, d2, d3, c1, c2, c3, sl, slsrc, sc,
    n_src, n_dst, k_src, k_dst, f_src, f_dst, n_hi, n_lo, gn_hi, gn_lo, small,
    hsend, hrecv, gsend, grecv, d1s, d1r, d2s, d2r, d3s, d3r, sls, slr, nsend, nrecv,
):
    gx = lax.axis_index("gx")
    gy = lax.axis_index("gy")
    yln, xcn = gxn // zn, gyn // yhn
    yn = yln * yhn
    zpos, xcpos = lax.rem(gx, zn), lax.rem(gy, xcn)
    ypos = (gy // xcn) * yln + gx // zn
    has_w, has_e = gx > 0, gx < gxn - 1
    has_s, has_n = gy > 0, gy < gyn - 1
    has_se = jnp.logical_and(has_e, has_s)
    has_nw = jnp.logical_and(has_w, has_n)
    by_y = lambda i: (gx, i)
    by_z = lambda i: ((gx // zn) * zn + i, gy)
    by_x = lambda i: (gx, (gy // xcn) * xcn + i)
    by_o = lambda i: (lax.rem(i, yln) * zn + zpos, (i // yln) * xcn + xcpos)

    for ref in (h_w, h_s, r_e, h_n, h_nw, n_dst, k_dst, small):
        ref[...] = jnp.zeros_like(ref)
    none = float(ainv.shape[0])
    f_dst[...] = jnp.full(f_dst.shape, none, F32)

    barrier = pltpu.get_barrier_semaphore()

    def greet(n, me, dev):
        def body(j, c):
            pl.semaphore_signal(barrier, inc=1, device_id=dev(lax.rem(me + j, n)), device_id_type=MESH)
            return c

        lax.fori_loop(1, n, body, 0, unroll=True)

    greet(gyn, gy, by_y)
    greet(zn, zpos, by_z)
    greet(yn, ypos, by_o)

    @pl.when(has_e)
    def _():
        pl.semaphore_signal(barrier, inc=1, device_id=(gx + 1, gy), device_id_type=MESH)

    @pl.when(has_w)
    def _():
        pl.semaphore_signal(barrier, inc=1, device_id=(gx - 1, gy), device_id_type=MESH)

    @pl.when(has_se)
    def _():
        pl.semaphore_signal(barrier, inc=1, device_id=(gx + 1, gy - 1), device_id_type=MESH)

    @pl.when(has_nw)
    def _():
        pl.semaphore_signal(barrier, inc=1, device_id=(gx - 1, gy + 1), device_id_type=MESH)

    lane = iota((16, 128), 1)
    row = iota((16, 128), 0)
    low = lane < 64
    low8 = iota((8, 128), 1) < 64

    for a in range(2):
        for b in range(4):
            s = a * 4 + b
            lam[s] = duals[:, a, b, :]
            res[s] = residual[:, a, b, :]
            kp = jnp.broadcast_to(active[a, b : b + 1, :].astype(F32), (16, 128))
            if a == 1:
                kp = jnp.where(jnp.logical_or(has_e, lane >= 64), kp, 0.0)
            if b == 3:
                kp = jnp.where(jnp.logical_or(has_n, lane < 64), kp, 0.0)
            keep[s] = kp
            dv[s] = kp * jnp.broadcast_to(scaling[a, b : b + 1, :], (16, 128))
            pv[s] = kp * direction[:, a, b, :]
            xv[a, b, :16] = dv[s] * res[s]
            xv[a, b, 16:] = pv[s]

    def dots(pairs):
        acc = jnp.zeros((16, 128), F32)
        for d, prod in enumerate(pairs):
            col = jnp.sum(jnp.sum(prod, axis=0), axis=1, keepdims=True)
            acc = jnp.where(lane == row + 16 * d, jnp.broadcast_to(col, (16, 128)), acc)
        return jnp.sum(acc, axis=0, keepdims=True)

    def column(line, d):
        picked = jnp.where(lane == row + 16 * d, jnp.broadcast_to(line, (16, 128)), 0.0)
        return jnp.broadcast_to(jnp.sum(picked, axis=1, keepdims=True), (16, 128))

    def stages(par):
        return (
            Group(xcn, xcpos, by_x, c1, d1.at[par], d1s, d1r.at[par]),
            Group(yn, ypos, by_o, c2, d2.at[par], d2s, d2r.at[par]),
            Group(zn, zpos, by_z, c3, d3.at[par], d3s, d3r.at[par]),
        )

    def total(group):
        group.wait()
        return jnp.sum(group.dst[...], axis=0)

    for a in range(2):
        for b in range(4):
            small[a * 4 + b : a * 4 + b + 1, :8] = slot[a, b : b + 1, :].astype(F32)
    small[8:9, :16] = prev_rho[...]
    spread = jnp.where(iota((128, 128), 0) == iota((128, 128), 1) % 8, 1.0, 0.0)
    each = jnp.dot(small[:8], spread, precision=lax.Precision.HIGHEST, preferred_element_type=F32)
    lane8 = iota((8, 128), 1)
    own_row = jnp.sum(jnp.where(lane8 // 8 == iota((8, 128), 0), each, 0.0), axis=0, keepdims=True)
    own_row = jnp.where(lane8[:1] < 64, own_row, none)
    f_src[...] = own_row

    slots = Group(gyn, gy, by_y, slsrc, sl, sls, slr)

    e = iota((256, 256), 0)
    orig = jnp.where(e < 64, e + 64, jnp.where(e < 128, e + 128, jnp.where(e < 192, e - 128, e - 64)))
    sign = jnp.where(e < 128, 1.0, -1.0)
    def turn(s):
        em = jnp.broadcast_to(emap[s // 4, s % 4 : s % 4 + 1, :], (256, 256))
        pt = jnp.where(em == orig, sign, 0.0).astype(BF16)
        sh, slo = split(schur[s])
        parts = dot(pt, dot_nt(sh, pt).astype(BF16)), dot(pt, dot_nt(slo, pt).astype(BF16))
        s_hi[s] = parts[0].astype(BF16)
        s_lo[s] = parts[1].astype(BF16)
        ch, cl = split(coupling[s])
        g_hi[s, :8] = dot_nt(ch, pt).astype(BF16)
        g_lo[s, :8] = dot_nt(cl, pt).astype(BF16)
        return parts

    def packed(first_half, second_half):
        return jnp.where(iota(first_half.shape, 1) < 64, pltpu.roll(first_half, 64, 1), second_half)

    zero, four = turn(0), turn(4)
    n_src[...] = packed((zero[0] + zero[1])[:, 128:], (four[0] + four[1])[:, 128:])
    corner = [(g_hi[s, :8].astype(F32) + g_lo[s, :8].astype(F32))[:, 128:] for s in (0, 4)]
    k_src[...] = packed(corner[0], corner[1])

    pl.semaphore_wait(
        barrier,
        (gyn - 1) + (zn - 1) + (yn - 1)
        + has_e.astype(jnp.int32) + has_w.astype(jnp.int32)
        + has_se.astype(jnp.int32) + has_nw.astype(jnp.int32),
    )
    south = (gx, gy - 1)
    early = (
        remote(f_src, f_dst, nsend.at[0], nrecv.at[0], south),
        remote(k_src, k_dst, nsend.at[1], nrecv.at[1], south),
        remote(n_src, n_dst, nsend.at[2], nrecv.at[2], south),
    )
    pl.when(has_s)(lambda: early[0].start())
    pl.when(has_s)(lambda: early[1].start())

    line_id = iota((1, 128), 1)
    sub, lan = iota((128, 128), 0), iota((128, 128), 1)
    square = lambda v: jnp.broadcast_to(v, (128, 128))
    width = ainv.shape[0]
    held = {}

    def number_corners():
        pl.when(has_s)(lambda: early[2].start())
        turn(1)
        turn(2)
        pl.when(has_n)(lambda: early[0].wait_recv())
        above = f_dst[...]
        ext = jnp.where(line_id < 64, own_row, jnp.where(
            line_id < 72, pltpu.roll(above, 64, 1), jnp.where(line_id < 80, pltpu.roll(above, 40, 1), none)
        ))
        ext_r = square(ext)
        ext_c = jnp.transpose(ext_r)
        seen = jnp.sum(jnp.where(jnp.logical_and(ext_c == ext_r, sub < lan), 1.0, 0.0), axis=0, keepdims=True)
        lead = jnp.where(jnp.logical_and(seen == 0.0, ext < none), 1.0, 0.0)
        lead_c = jnp.transpose(square(lead))
        rank = jnp.sum(jnp.where(ext_c < ext_r, lead_c, 0.0), axis=0, keepdims=True)
        rank_c = jnp.transpose(square(rank))
        chosen = jnp.sum(jnp.where(rank_c == lan.astype(F32), lead_c * (ext_c - none), 0.0), axis=0, keepdims=True)
        slots.start(chosen + none)
        pick = jnp.where(jnp.logical_and(square(rank) == (sub % 64).astype(F32), ext_r < none), 1.0, 0.0)
        for s in (3, 5, 6, 7):
            turn(s)
        for s in range(8):
            mine = jnp.where(lan // 8 == s, pick, 0.0).astype(BF16)
            for ref in (g_hi, g_lo):
                rows = jnp.concatenate([ref[s, :8].astype(F32)] * 16, axis=0).astype(BF16)
                ref[s] = dot(mine, rows).astype(BF16)
        pl.when(has_n)(lambda: early[1].wait_recv())
        upper = jnp.concatenate([k_dst[...]] * 16, axis=0)
        halves = []
        for a in range(2):
            mine = jnp.where(lan // 8 == 8 + a, pick, 0.0).astype(BF16)
            halves.append([dot(mine, part) for part in split(upper)])
        gn_hi[...] = jnp.where(lan < 64, halves[0][0], halves[1][0]).astype(BF16)
        gn_lo[...] = jnp.where(lan < 64, halves[0][1], halves[1][1]).astype(BF16)
        corners = jnp.where(
            jnp.concatenate([ext_c] * (width // 128), axis=1) == iota((128, width), 1).astype(F32), 1.0, 0.0
        )
        held["hot"] = jnp.where(jnp.logical_and(sub < 64, square(lead) > 0.0), pick, 0.0), corners

    def own_inverse():
        own_hot = dot(held["hot"][0].astype(BF16), held["hot"][1].astype(BF16)).astype(BF16)
        ah, al = split(ainv[...])
        held["rows"] = dot(own_hot, ah).astype(BF16), dot(own_hot, al).astype(BF16)

    def upper_block():
        pl.when(has_n)(lambda: early[2].wait_recv())
        nh, nl = split(n_dst[...])
        n_hi[...] = nh
        n_lo[...] = nl

    def region_inverse():
        tall = iota((width, 128), 0).astype(F32)
        slots.wait()
        yh, yl = held["rows"]
        for pair in range(gyn // 2):
            both = jnp.where(low8[:1], sl[2 * pair], pltpu.roll(sl[2 * pair + 1], 64, 1))
            hot = jnp.where(tall == jnp.broadcast_to(both, (width, 128)), 1.0, 0.0).astype(BF16)
            cols = slice(pair * 128, pair * 128 + 128)
            m_hi[:, cols] = dot(yh, hot).astype(BF16)
            m_lo[:, cols] = dot(yl, hot).astype(BF16)

    def halo(par, rows):
        r = pl.ds(0, rows)
        return (
            remote(xv.at[1, :, r], h_w.at[par, :, r], hsend.at[0], hrecv.at[par, 0], (gx + 1, gy)),
            remote(xv.at[:, 3, r], h_s.at[par, :, r], hsend.at[1], hrecv.at[par, 1], (gx, gy + 1)),
            remote(xv.at[:, 0, r], h_n.at[par, :, r], hsend.at[2], hrecv.at[par, 2], (gx, gy - 1)),
            remote(xv.at[1, 0, r], h_nw.at[par, r], hsend.at[3], hrecv.at[par, 3], (gx + 1, gy - 1)),
            remote(wn.at[:, r], r_e.at[par, :, r], hsend.at[4], hrecv.at[par, 4], (gx - 1, gy)),
        )

    sends = (has_e, has_n, has_s, has_se, has_w)
    receives = (has_w, has_s, has_n, has_nw, has_e)

    def each_of(copies, which, go, verb):
        for i in which:
            pl.when(go[i])(lambda i=i: getattr(copies[i], verb)())

    def fold(v):
        return v[: v.shape[0] // 2] + v[v.shape[0] // 2 :]

    def three(both, hi, high, low_part, product):
        return fold(product(both, high)) + product(hi, low_part)

    def apply(par, fields, line, hooks):
        nothing = lambda: None
        rows = 16 * fields
        low = iota((rows, 128), 1) < 64
        copies = halo(par, rows)
        coarse = Group(
            gyn, gy, by_y, ct.at[: 8 * fields], g1.at[par, :, : 8 * fields], gsend, grecv.at[par]
        )
        groups = stages(par) if line is not None else ()
        each_of(copies, (0, 1, 2, 3), sends, "start")
        if groups:
            groups[0].start(line)
        hooks.get("corners", nothing)()
        each_of(copies, (0,), receives, "wait_recv")
        if groups:
            groups[1].start(total(groups[0]))
        hi, lo = split(packed(xv[0, 3, :rows], xv[1, 3, :rows]))
        v2 = three(jnp.concatenate([hi, lo], axis=0), hi, gn_hi[...], gn_lo[...], dot_nt)
        for a in range(2):
            for b in range(4):
                s = a * 4 + b
                west = h_w[par, b, :rows] if a == 0 else xv[0, b, :rows]
                beside = jnp.where(low, west, 0.0 if b == 0 else xv[a, b - 1, :rows])
                hi, lo = split(jnp.concatenate([xv[a, b, :rows], beside], axis=1))
                both = jnp.concatenate([hi, lo], axis=0)
                lhs[s, : 2 * rows] = both
                v2 = v2 + three(both, hi, g_hi[s], g_lo[s], dot_nt)
        coarse.start(jnp.concatenate(
            [jnp.where(low8, v2[16 * f : 16 * f + 8], v2[16 * f + 8 : 16 * f + 16]) for f in range(fields)], axis=0
        ))

        def local(s):
            wk[s, :rows] = three(lhs[s, : 2 * rows], lhs[s, :rows], s_hi[s], s_lo[s], dot)

        for s in (1, 2, 3, 5, 6, 7):
            local(s)
        hooks.get("inverse", nothing)()
        if groups:
            groups[2].start(total(groups[1]))
        each_of(copies, (1, 2, 3), receives, "wait_recv")
        for a in range(2):
            s = a * 4
            west = h_w[par, 0, :rows] if a == 0 else xv[0, 0, :rows]
            hi, lo = split(jnp.where(low, west, h_s[par, a, :rows]))
            lhs[s, :rows, 128:] = hi
            lhs[s, rows : 2 * rows, 128:] = lo
            local(s)
        hooks.get("upper", nothing)()
        above = [
            jnp.concatenate([
                h_n[par, a, :rows],
                jnp.where(low, h_nw[par, :rows] if a == 0 else h_n[par, 0, :rows], xv[a, 3, :rows]),
            ], axis=1)
            for a in range(2)
        ]
        hi, lo = split(jnp.concatenate(above, axis=0))
        both = three(jnp.concatenate([hi, lo], axis=0), hi, n_hi[...], n_lo[...], dot)
        upper = jnp.where(low, both[:rows], both[rows:])
        hooks.get("region", nothing)()
        coarse.wait()
        pieces = []
        for pair in range(gyn // 2):
            parts = []
            for f in range(fields):
                one, two = g1[par, 2 * pair, 8 * f : 8 * f + 8], g1[par, 2 * pair + 1, 8 * f : 8 * f + 8]
                parts.append(jnp.where(low8, one, pltpu.roll(two, 64, 1)))
                parts.append(jnp.where(low8, pltpu.roll(one, 64, 1), two))
            pieces.append(jnp.concatenate(parts, axis=0))
        hi, lo = split(jnp.concatenate(pieces, axis=1))
        back = three(jnp.concatenate([hi, lo], axis=0), hi, m_hi[...], m_lo[...], dot_nt)
        bhi, blo = split(back)
        bhl = jnp.concatenate([bhi, blo], axis=0)
        for s in range(8):
            full = wk[s, :rows] + three(bhl, bhi, g_hi[s], g_lo[s], dot)
            wk[s, :rows] = full
            if s < 4:
                wn[s, :rows] = full[:, 128:]
            if s == 3:
                each_of(copies, (4,), sends, "start")
        upper = upper + three(bhl, bhi, gn_hi[...], gn_lo[...], dot)
        summed = total(groups[2]) if groups else None
        each_of(copies, (4,), receives, "wait_recv")
        result = []
        for a in range(2):
            for b in range(4):
                s = a * 4 + b
                east = r_e[par, b, :rows] if a == 1 else wk[4 + b, :rows, 128:]
                if b < 3:
                    north = wk[s + 1, :rows, 128:]
                else:
                    north = pltpu.roll(upper, 64, 1) if a == 0 else upper
                got = wk[s, :rows, :128] + jnp.where(low, east, north)
                result.append(got * jnp.concatenate([keep[s]] * fields, axis=0))
        each_of(copies, (0, 1, 2, 3, 4), sends, "wait_send")
        for group in groups + (coarse,):
            group.finish()
        return jnp.stack(result), summed

    def residual_products():
        z = dv[...] * res[...]
        return [res[...] * z, z * wv[...], z * qv[...]]

    def step_of(line):
        rho = column(line, 0)
        beta = rho / sc[0]
        pq = column(line, 1) + beta * (2.0 * column(line, 2) + beta * sc[1])
        alpha = rho / pq
        sc[0] = rho
        sc[1] = pq
        return beta, alpha, dv[...] * res[...] + beta * pv[...]

    def advance(got, summed):
        beta, alpha, p = step_of(summed)
        pv[...] = p
        q = wv[...] + beta * qv[...]
        t = got + beta * tv[...]
        qv[...] = q
        tv[...] = t
        lam[...] += alpha * p
        res[...] -= alpha * q
        w = wv[...] - alpha * t
        wv[...] = w
        xv[:, :, :16] = (dv[...] * w).reshape(2, 4, 16, 128)
        return dots(residual_products())

    got, _ = apply(0, 2, None, {
        "corners": number_corners, "inverse": own_inverse, "upper": upper_block, "region": region_inverse,
    })
    slots.finish()
    for copy in early:
        pl.when(has_s)(lambda copy=copy: copy.wait_send())
    w, q = got[:, :16], got[:, 16:]
    wv[...] = w
    qv[...] = q
    xv[:, :, :16] = (dv[...] * w).reshape(2, 4, 16, 128)
    xv[:, :, 16:] = (dv[...] * q).reshape(2, 4, 16, 128)
    line = dots(residual_products() + [pv[...] * q])
    got, summed = apply(1, 2, line, {})
    tv[...] = got[:, 16:]
    sc[0] = column(small[8:9], 0)
    sc[1] = column(summed, 3)
    line = advance(got[:, :16], summed)

    def round_body(i, line):
        got, summed = apply(lax.rem(i, 2), 1, line, {})
        return advance(got, summed)

    line = lax.fori_loop(2, iters, round_body, line)

    last = stages(iters % 2)
    last[0].start(line)
    last[1].start(total(last[0]))
    last[2].start(total(last[1]))
    beta, alpha, p = step_of(total(last[2]))
    new_l = lam[...] + alpha * p
    new_r = res[...] - alpha * (wv[...] + beta * qv[...])
    for a in range(2):
        for b in range(4):
            s = a * 4 + b
            out_l[:, a, b, :] = new_l[s]
            out_r[:, a, b, :] = new_r[s]
            out_p[:, a, b, :] = p[s]
    for group in last:
        group.finish()


def shards(gxn, gyn, zn, yhn, duals, residual, direction, prev_rho, schur, coupling, ainv, emap, slot, active, scaling):
    yn = gxn // zn * yhn
    vmem = pl.BlockSpec(memory_space=pltpu.VMEM)
    field = jax.ShapeDtypeStruct(duals.shape, F32)
    tiles = lambda *lead: pltpu.VMEM(lead + (16, 128), F32)
    pair = lambda *lead: pltpu.VMEM(lead + (32, 128), F32)
    line = lambda *lead: pltpu.VMEM(lead + (1, 128), F32)
    dma = lambda *shape: pltpu.SemaphoreType.DMA(shape)
    return pl.pallas_call(
        functools.partial(kernel, gxn, gyn, zn, yhn, 6),
        out_shape=(field, field, field),
        in_specs=[vmem] * 11,
        out_specs=(vmem, vmem, vmem),
        scratch_shapes=[
            pltpu.VMEM((8, 256, 256), BF16), pltpu.VMEM((8, 256, 256), BF16),
            pltpu.VMEM((8, 128, 256), BF16), pltpu.VMEM((8, 128, 256), BF16),
            pltpu.VMEM((128, 64 * gyn), BF16), pltpu.VMEM((128, 64 * gyn), BF16),
            pltpu.VMEM((8, 64, 256), BF16),
            tiles(8), tiles(8), tiles(8), tiles(8), tiles(8), tiles(8), pair(2, 4), tiles(8), tiles(8),
            pltpu.VMEM((8, 32, 256), F32), pair(4),
            pair(2, 4), pair(2, 2), pair(2, 4), pair(2, 2), pair(2),
            pltpu.VMEM((2, gyn, 16, 128), F32), pltpu.VMEM((16, 128), F32),
            line(2, gyn // yhn), line(2, yn), line(2, zn), line(), line(), line(),
            line(gyn), line(), tiles(2),
            pltpu.VMEM((256, 128), F32), pltpu.VMEM((256, 128), F32), pltpu.VMEM((8, 128), F32), pltpu.VMEM((8, 128), F32),
            line(), line(),
            pltpu.VMEM((256, 128), BF16), pltpu.VMEM((256, 128), BF16), pltpu.VMEM((128, 128), BF16), pltpu.VMEM((128, 128), BF16),
            pltpu.VMEM((16, 128), F32),
            dma(5), dma(2, 5), dma(gyn), dma(2, gyn),
            dma(gyn // yhn), dma(2, gyn // yhn), dma(yn), dma(2, yn), dma(zn), dma(2, zn), dma(gyn), dma(gyn), dma(3), dma(3),
        ],
        compiler_params=pltpu.CompilerParams(collective_id=0, has_side_effects=True),
    )(duals, residual, direction, prev_rho.reshape(1, 16), schur.reshape(8, 256, 256), coupling.reshape(8, 8, 256), ainv[0], emap, slot, active, scaling)


def solution(mesh):
    gxn, gyn = mesh.shape["gx"], mesh.shape["gy"]
    zn = 8 if gxn % 8 == 0 else 2
    yhn = 2
    grid = P(None, "gx", "gy", None)
    cells = P("gx", "gy", None)
    return jax.shard_map(
        functools.partial(shards, gxn, gyn, zn, yhn),
        mesh=mesh,
        in_specs=(
            grid, grid, grid, P(), P("gx", "gy", None, None), P("gx", "gy", None, None), P("gx", None, None),
            cells, cells, cells, cells,
        ),
        out_specs=(grid, grid, grid),
        check_vma=False,
    )
```

time: 169 us -> 133 us (0.79)
  Pallas kernels: 161 us -> 127 us
    pallas_call x1, Pallas kernels: 161 us -> 127 us  [shards(): pl.pallas_call(functools.partial(kernel, gxn, gyn, zn, yhn, 6), out_shape...]
where the time goes in v2:
time: 133 us; the launch traced here: 132 us
  Pallas kernels  127 us (95%)
  local copies, waits for them, and re-layouts  4.42 us (3%)
    pallas_call x1, Pallas kernels, shards(): pl.pallas_call(functools.partial(kernel, gxn, gyn, zn, yhn, 6), out_shape...  127 us
    unnamed x3, local copies, waits for them, and re-layouts  4.42 us

profile of v2, /device:TPU:1, one launch (start us, length us, event | category | flops | bytes accessed | tf_op | source)
XLA Modules:
  0.0 132.0 jit_solution(15126133062211478212)
XLA Ops:
  0.6 126.9 %shard_map.130 = (f32[16,2,4,128]{3,2,1,0:T(4,128)}, f32[16,2,4,128]{3,2,1,0:T(4,128)}, f32[16,2,4,128]{3,2,1,0:T(4,128)}) custom-call(f32[16,2,4,128]{3,2,1,0:T(4,128)} %duals.1, f32[16,2,4,128]{3,2,1,0:T(4,128)} %residual.1, f32[16,2,4,128]{3,2,1,0:T(4,128)} %direction.1, f32[1,16]{1,0:T(1,128)} %bitcast.7, f32[8,256,256]{2,1,0:T(8,128)} %bitcast.4, ...), custom_call_target="tpu_custom_call" | custom-call | tf_op jit(solution)/shard_map/pallas_call | solution.py:487
  127.5 1.5 %copy.17 = f32[16,2,4,128]{3,2,1,0:T(4,128)} copy(f32[16,2,4,128]{3,2,1,0:T(4,128)} %get-tuple-element.6) | data formatting | bytes 131072
  129.0 1.5 %copy.18 = f32[16,2,4,128]{3,2,1,0:T(4,128)} copy(f32[16,2,4,128]{3,2,1,0:T(4,128)} %get-tuple-element.7) | data formatting | bytes 131072
  130.5 1.5 %copy.19 = f32[16,2,4,128]{3,2,1,0:T(4,128)} copy(f32[16,2,4,128]{3,2,1,0:T(4,128)} %get-tuple-element.8) | data formatting | bytes 131072
